TPU v7x, 256 devices: a whole 4x4x8 slice. The times are simulated.
256 devices in a mesh: req: 16 (over y, x), kv: 8 (over z), blk: 2 (over core).
Axes of the slice: x: 4, y: 4, z: 8, core: 2. Of those that a mesh axis runs over, the one named last changes fastest.
Arguments:
- x_resid: bfloat16 [16, 256, 5120], P('req', ('kv', 'blk')), may hold values from -54 to 54
- q_new: bfloat16 [16, 256, 4096], P('req', None, 'kv'), may hold values from -36 to 36
- k_new: bfloat16 [16, 256, 1024], P('req', None, 'kv'), may hold values from -6 to 12
- v_new: bfloat16 [16, 256, 1024], P('req', None, 'kv'), may hold values from -24 to 24
- k_cache: bfloat16 [16, 8, 64, 128, 128], P('req', 'kv', 'blk'), may hold values from -6 to 12
- v_cache: bfloat16 [16, 8, 64, 128, 128], P('req', 'kv', 'blk'), may hold values from -24 to 24
- cache_len: int32 [16], P('req'), may hold values from 1 to 7936, as said below
- page_table: int32 [16, 64], P('req'), may hold values from 0 to 63, as said below
- wo: bfloat16 [4096, 5120], P(('kv', 'blk')), may hold values from -0.09375 to 0.09375
- norm_gain: bfloat16 [5120], replicated, may hold values from 0.099609375 to 1.8984375
- w_gate: bfloat16 [5120, 7168], P('req', ('kv', 'blk')), may hold values from -0.078125 to 0.078125
- w_up: bfloat16 [5120, 7168], P('req', ('kv', 'blk')), may hold values from -0.078125 to 0.078125
- w_down: bfloat16 [7168, 5120], P(('kv', 'blk'), 'req'), may hold values from -0.0625 to 0.0625
Outputs:
- layer_out: bfloat16 [16, 256, 5120], P('req', ('kv', 'blk'))
- k_cache_out: bfloat16 [16, 8, 64, 128, 128], P('req', 'kv', 'blk')
- v_cache_out: bfloat16 [16, 8, 64, 128, 128], P('req', 'kv', 'blk')
Inputs may be any that keep to these rules, and one draw needn't show every extreme that they name: `cache_len`: at least one request has the largest length. `page_table`: each row is a permutation of 0 to 63.
All inputs are finite; a program needn't handle non-finite values.
Results may differ from a plain program's by a relative error of at most 0.0095.
Values may be sent and summed in bfloat16 or wider, within the bound.
A program may use at most 128 MiB of HBM per device.

v0:
```python
import math
import jax
import jax.numpy as jnp
from jax import lax
from jax.sharding import PartitionSpec as P


def combined_all(part, axis, combine):
    gathered = jax.tree.map(lambda a: lax.all_gather(a, axis), part)

    def take(source):
        return jax.tree.map(lambda a: lax.dynamic_index_in_dim(a, source, 0, False), gathered)

    return lax.fori_loop(
        1, lax.axis_size(axis), lambda source, state: combine(state, take(source)), take(0)
    )


def rotate(field, positions):
    half_width = field.shape[-1] // 2
    pair_index = jnp.arange(half_width, dtype=jnp.float32)
    frequency = jnp.power(1000000.0, -2.0 * pair_index / field.shape[-1])
    angles = positions.astype(jnp.float32)[:, None] * frequency[None, :]
    cosine = jnp.cos(angles)
    sine_part = jnp.sin(angles)
    lower_half = field[..., :half_width]
    upper_half = field[..., half_width:]
    return jnp.concatenate(
        [
            lower_half * cosine - upper_half * sine_part,
            upper_half * cosine + lower_half * sine_part,
        ],
        axis=-1,
    )


def merge_parts(first_part, second_part):
    max_first, total_first, out_first = first_part
    max_second, total_second, out_second = second_part
    overall = jnp.maximum(max_first, max_second)
    factor_first = jnp.exp(max_first - overall)
    factor_second = jnp.exp(max_second - overall)
    return (
        overall,
        factor_first * total_first + factor_second * total_second,
        factor_first[..., None] * out_first + factor_second[..., None] * out_second,
    )


def fetch_down(w_down):
    return lax.all_gather(w_down, "req", axis=1, tiled=True)


def rms_rows(rows, norm_gain):
    return (
        rows
        * lax.rsqrt(jnp.mean(rows * rows, axis=-1, keepdims=True) + 1e-05)
        * norm_gain.astype(jnp.float32)
    ).astype(jnp.bfloat16)


def on_device(
    x_resid,
    q_new,
    k_new,
    v_new,
    k_cache,
    v_cache,
    cache_len,
    page_table,
    wo,
    norm_gain,
    w_gate,
    w_up,
    w_down,
):
    blk_count = lax.axis_size("blk")
    blk_id = lax.axis_index("blk")
    new_tokens = q_new.shape[1]
    head_dim = k_new.shape[2]
    group_size = q_new.shape[2] // head_dim
    slot_count = k_cache.shape[2]
    page_size = k_cache.shape[3]
    page_total = page_table.shape[1]
    length = cache_len[0]
    positions = length + jnp.arange(new_tokens, dtype=jnp.int32)
    query_heads = rotate(
        q_new[0].reshape(new_tokens, group_size, head_dim).astype(jnp.float32).transpose(1, 0, 2),
        positions,
    ).astype(jnp.bfloat16)
    fresh_keys = rotate(k_new[0].astype(jnp.float32), positions).astype(jnp.bfloat16)
    page_ids = jnp.arange(page_total, dtype=jnp.int32)
    physical = blk_id * slot_count + jnp.arange(slot_count, dtype=jnp.int32)
    logical = jnp.sum(
        jnp.where(page_table[0][None, :] == physical[:, None], page_ids[None, :], 0), axis=1
    )
    slot_position = (
        logical[:, None] * page_size + jnp.arange(page_size, dtype=jnp.int32)[None, :]
    ).reshape(slot_count * page_size)
    new_index = slot_position - length
    is_new = (new_index >= 0) & (new_index < new_tokens)
    chosen = jnp.clip(new_index, 0, new_tokens - 1)
    key_rows = jnp.where(
        is_new[:, None], fresh_keys[chosen], k_cache[0, 0].reshape(slot_count * page_size, head_dim)
    )
    value_rows = jnp.where(
        is_new[:, None], v_new[0][chosen], v_cache[0, 0].reshape(slot_count * page_size, head_dim)
    )
    scores = jnp.einsum(
        "qd,sd->qs",
        query_heads.reshape(group_size * new_tokens, head_dim),
        key_rows,
        preferred_element_type=jnp.float32,
    ) * (1.0 / math.sqrt(head_dim))
    scores = scores.reshape(group_size, new_tokens, slot_count * page_size)
    allowed = slot_position[None, None, :] <= positions[None, :, None]
    masked = jnp.where(allowed, scores, -1e30)
    block_max = jnp.max(masked, axis=-1)
    weights = jnp.where(allowed, jnp.exp(masked - block_max[..., None]), 0.0).astype(jnp.bfloat16)
    block_total = jnp.sum(weights.astype(jnp.float32), axis=-1)
    block_out = jnp.einsum("gcs,sd->gcd", weights, value_rows, preferred_element_type=jnp.float32)
    merged = combined_all((block_max, block_total, block_out), "blk", merge_parts)
    attn = (merged[2] / merged[1][..., None]).astype(jnp.bfloat16)
    per_core = group_size // blk_count
    mine = lax.dynamic_slice_in_dim(attn, blk_id * per_core, per_core, 0)
    mine_rows = mine.transpose(1, 0, 2).reshape(new_tokens, per_core * head_dim)
    token_rows = x_resid.shape[1]
    row_start = lax.axis_index(("kv", "blk")) * token_rows
    partial_value = jnp.dot(mine_rows, wo, preferred_element_type=jnp.float32)
    own_part = lax.dynamic_slice_in_dim(partial_value, row_start, token_rows, 0) + x_resid[
        0
    ].astype(jnp.float32)
    contrib = lax.dynamic_update_slice_in_dim(partial_value, own_part, row_start, 0)
    resid = lax.psum(contrib, ("kv", "blk"))
    normed = rms_rows(resid, norm_gain)
    own_resid = lax.dynamic_slice_in_dim(resid, row_start, token_rows, 0)
    gate_val = jnp.dot(
        normed,
        lax.all_gather(w_gate, "req", axis=0, tiled=True),
        preferred_element_type=jnp.float32,
    )
    up_val = jnp.dot(
        normed, lax.all_gather(w_up, "req", axis=0, tiled=True), preferred_element_type=jnp.float32
    )
    hidden = (jax.nn.silu(gate_val) * up_val).astype(jnp.bfloat16)
    down_full = fetch_down(w_down)
    mlp_rows = lax.psum_scatter(
        jnp.dot(hidden, down_full, preferred_element_type=jnp.float32).astype(jnp.bfloat16),
        ("kv", "blk"),
        scatter_dimension=0,
        tiled=True,
    ).astype(jnp.float32)
    layer_out = (own_resid + mlp_rows).astype(jnp.bfloat16)[None]
    return (layer_out, key_rows.reshape(k_cache.shape), value_rows.reshape(v_cache.shape))


def solution(mesh):
    in_specs = (
        P("req", ("kv", "blk"), None),
        P("req", None, "kv"),
        P("req", None, "kv"),
        P("req", None, "kv"),
        P("req", "kv", "blk", None, None),
        P("req", "kv", "blk", None, None),
        P("req"),
        P("req", None),
        P(("kv", "blk"), None),
        P(),
        P("req", ("kv", "blk")),
        P("req", ("kv", "blk")),
        P(("kv", "blk"), "req"),
    )
    out_specs = (
        P("req", ("kv", "blk"), None),
        P("req", "kv", "blk", None, None),
        P("req", "kv", "blk", None, None),
    )
    return jax.shard_map(
        on_device, mesh=mesh, in_specs=in_specs, out_specs=out_specs, check_vma=False
    )
```

profile of v0, /device:TPU:2, one launch (start us, length us, event | category | flops | bytes accessed | tf_op | source)
XLA Modules:
  0.0 365.1 jit_solution(288112992523952814)
XLA Ops:
  8.9 0.9 copy.31
  9.9 0.3 multiply_cosine_fusion
  10.3 0.8 select_reduce_fusion
  11.4 1.9 reshape.295
  13.3 1.3 copy.30
  14.8 15.0 %gather_fusion = bf16[4096,128]{1,0:T(8,128)(2,1)} fusion(bf16[256,128]{1,0:T(8,128)(2,1)S(1)} %copy.32, s32[4096]{0:T(1024)S(1)} %broadcast_clamp_fusion), kind=kCustom, calls=%fused_computation | custom fusion | bytes 2113536 | tf_op jit(solution)/shard_map/gather | solution.py:104
  29.8 15.0 %gather_fusion.1 = bf16[4096,128]{1,0:T(8,128)(2,1)} fusion(bf16[256,128]{1,0:T(8,128)(2,1)S(1)} %bitcast.87, s32[4096]{0:T(1024)S(1)} %broadcast_clamp_fusion), kind=kCustom, calls=%fused_computation.1 | custom fusion | bytes 2113536 | tf_op jit(solution)/shard_map/gather | solution.py:107
  44.9 0.6 broadcast_compare_fusion
  45.6 3.6 bitcast_select_fusion.2
  49.2 3.7 %fusion.1 = (f32[1024]{0:T(1024)S(1)}, f32[1024,4096]{1,0:T(8,128)S(1)}) fusion(pred[256,4096]{1,0:T(8,128)(4,1)S(1)} %broadcast_compare_fusion, bf16[4096,128]{1,0:T(8,128)(2,1)S(1)} %bitcast_select_fusion.2, bf16[1024,64]{0,1:T(8,128)(2,1)S(1)} %bitcast.95, bf16[1024,64]{0,1:T(8,128)(2,1)S(1)} %bitcast.94), kind=kOutput, calls=%fused_computation.6 | convolution fusion | flops 1086848000 | bytes 19140608 | tf_op jit(solution)/shard_map/qd,sd->qs/dot_general | solution.py:109
  52.9 6.7 %convert_reduce_fusion = (f32[1024]{0:T(1024)S(1)}, bf16[1024,4096]{1,0:T(8,128)(2,1)S(1)}) fusion(f32[1024]{0:T(1024)S(1)} %get-tuple-element.46, f32[1024,4096]{1,0:T(8,128)S(1)} %get-tuple-element.47, pred[256,4096]{1,0:T(8,128)(4,1)S(1)} %broadcast_compare_fusion), kind=kLoop, calls=%fused_computation.5 | loop fusion | flops 29359104 | bytes 26222592 | tf_op jit(solution)/shard_map/reduce_sum | solution.py:120
  59.7 1.5 broadcast_select_fusion
  61.2 1.0 copy-done.6
  62.2 3.2 fusion.34
  65.4 1.8 all_gather.32
  67.3 2.0 all_gather.28
  69.3 13.5 %all-gather.12.cloned.1.call-done = f32[8,256,128]{2,1,0:T(8,128)} async-done(((f32[4,256,128]{2,1,0:T(8,128)}), f32[8,256,128]{2,1,0:T(8,128)}) %all-gather.12.cloned.1.call-update) | async-done | bytes 1048592 | tf_op jit(solution)/shard_map/all_gather | solution.py:9
  82.8 1.3 fusion.33
  84.1 0.8 copy.37
  85.1 1.0 divide_convert_fusion
  86.2 3.2 fusion.35
  89.4 1.7 fusion.8
  91.2 0.5 all-gather.6.cloned.1.call-update
  91.7 0.5 all-gather.10.cloned.1.call-update
  92.3 0.5 all-gather.8.cloned.1.call-update
  92.9 126.8 %all-reduce.2.cloned.1.call-done = f32[256,5120]{1,0:T(8,128)} async-done(((f32[256,5120]{1,0:T(8,128)}), f32[256,5120]{1,0:T(8,128)}) %all-reduce.2.cloned.1.call-update) | async-done | bytes 5242896 | tf_op jit(solution)/shard_map/psum | solution.py:134
  219.8 2.9 multiply_reduce_fusion
  222.7 6.2 %fusion.29 = f32[256,448]{0,1:T(8,128)S(1)} fusion(bf16[5120,448]{1,0:T(8,128)(2,1)} %all-gather.6.cloned.1.call-done, f32[256,5120]{1,0:T(8,128)} %all-reduce.2.cloned.1.call-done, f32[5120]{0:T(1024)S(1)} %convert_element_type.69, f32[256]{0:T(256)S(1)} %add_rsqrt_fusion), kind=kOutput, calls=%fused_computation.74 | convolution fusion | flops 1178337280 | bytes 10310656 | tf_op jit(solution)/shard_map/dot_general | solution.py:137
  228.9 53.8 %all-gather.8.cloned.1.call-done = bf16[5120,448]{1,0:T(8,128)(2,1)} async-done(((bf16[320,448]{1,0:T(8,128)(2,1)}), bf16[5120,448]{1,0:T(8,128)(2,1)}) %all-gather.8.cloned.1.call-update) | async-done | bytes 4587536 | tf_op jit(solution)/shard_map/all_gather | solution.py:143
  282.8 12.4 %convolution_convert_fusion = bf16[256,5120]{1,0:T(8,128)(2,1)} fusion(bf16[448,5120]{0,1:T(8,128)(2,1)} %all-gather.10.cloned.1.call-done, bf16[5120,448]{1,0:T(8,128)(2,1)} %all-gather.8.cloned.1.call-done, f32[256,448]{0,1:T(8,128)S(1)} %fusion.29, f32[256,5120]{1,0:T(8,128)} %all-reduce.2.cloned.1.call-done, f32[5120]{0:T(1024)S(1)} %convert_element_type.69, ...), kind=kOutput, calls=%fused_computation.7 | convolution fusion | flops 2354741248 | bytes 17519616 | tf_op jit(solution)/shard_map/dot_general | solution.py:148
  295.2 60.8 %reduce-scatter.2.cloned.1.call-done = bf16[16,5120]{1,0:T(8,128)(2,1)} async-done(((bf16[256,5120]{1,0:T(8,128)(2,1)}), bf16[16,5120]{1,0:T(8,128)(2,1)}) %reduce-scatter.2.cloned.1.call-update) | async-done | bytes 163856 | tf_op jit(solution)/shard_map/reduce_scatter | solution.py:147
  356.0 1.8 fusion.14
  (54 shorter events, 1.2 us)
Async XLA Ops:
  8.0 78.2 %copy-start = (bf16[256,5120]{1,0:T(8,128)(2,1)S(1)}, bf16[256,5120]{1,0:T(8,128)(2,1)}, u32[]{:S(2)}) copy-start(bf16[256,5120]{1,0:T(8,128)(2,1)} %param.21) | copy-start | bytes 7864324
  8.0 74.8 %all-gather.12.cloned.1.call-start = ((), (), s32[]{:S(2)}) async-start(), calls=%async_computation.6 | async-start | bytes 1572864 | tf_op jit(solution)/shard_map/all_gather | solution.py:9
  14.6 15.2 %copy-start.1 = (bf16[1,256,128]{2,1,0:T(8,128)(2,1)S(1)}, bf16[1,256,128]{2,1,0:T(8,128)(2,1)}, u32[]{:S(2)}) copy-start(bf16[1,256,128]{2,1,0:T(8,128)(2,1)} %param.16) | copy-start | bytes 196612
  52.9 6.8 %copy-start.2 = (bf16[4096,128]{1,0:T(8,128)(2,1)S(1)}, bf16[4096,128]{1,0:T(8,128)(2,1)}, u32[]{:S(2)}) copy-start(bf16[4096,128]{1,0:T(8,128)(2,1)} %gather_fusion) | copy-start | bytes 3145732
  52.9 6.8 %copy-start.3 = (bf16[4096,128]{1,0:T(8,128)(2,1)S(1)}, bf16[4096,128]{1,0:T(8,128)(2,1)}, u32[]{:S(2)}) copy-start(bf16[4096,128]{1,0:T(8,128)(2,1)} %gather_fusion.1) | copy-start | bytes 3145732
  52.9 6.8 %copy-start.4 = (bf16[1,1,32,128,128]{4,3,2,1,0:T(8,128)(2,1)S(1)}, bf16[1,1,32,128,128]{4,3,2,1,0:T(8,128)(2,1)}, u32[]{:S(2)}) copy-start(bf16[1,1,32,128,128]{4,3,2,1,0:T(8,128)(2,1)} %param.17) | copy-start | bytes 3145732
  52.9 6.8 %copy-start.5 = (bf16[1,1,32,128,128]{4,3,2,1,0:T(8,128)(2,1)S(1)}, bf16[1,1,32,128,128]{4,3,2,1,0:T(8,128)(2,1)}, u32[]{:S(2)}) copy-start(bf16[1,1,32,128,128]{4,3,2,1,0:T(8,128)(2,1)} %param.18) | copy-start | bytes 3145732
  61.2 1.0 copy-start.6
  65.4 154.4 %all-reduce.2.cloned.1.call-start = ((), (), s32[]{:S(2)}) async-start(), calls=%async_computation.1 | async-start | bytes 10485760 | tf_op jit(solution)/shard_map/psum | solution.py:134
  85.0 4.4 %copy-start.7 = (bf16[1,16,5120]{2,1,0:T(8,128)(2,1)S(1)}, bf16[1,16,5120]{2,1,0:T(8,128)(2,1)}, u32[]{:S(2)}) copy-start(bf16[1,16,5120]{2,1,0:T(8,128)(2,1)} %param.13) | copy-start | bytes 491524
  89.4 3.6 copy-start.8
  91.1 131.6 %all-gather.6.cloned.1.call-start = ((), (), s32[]{:S(2)}) async-start(), calls=%async_computation.2 | async-start | bytes 5570560 | tf_op jit(solution)/shard_map/all_gather | solution.py:139
  91.7 137.2 %all-gather.10.cloned.1.call-start = ((), (), s32[]{:S(2)}) async-start(), calls=%async_computation.4 | async-start | bytes 5570560 | tf_op jit(solution)/shard_map/all_gather | solution.py:51
  92.3 190.5 %all-gather.8.cloned.1.call-start = ((), (), s32[]{:S(2)}) async-start(), calls=%async_computation.3 | async-start | bytes 5570560 | tf_op jit(solution)/shard_map/all_gather | solution.py:143
  92.9 263.1 %reduce-scatter.2.cloned.1.call-start = ((), (), s32[]{:S(2)}) async-start(), calls=%async_computation.5 | async-start | bytes 2785280 | tf_op jit(solution)/shard_map/reduce_scatter | solution.py:147
Sparse Core Ops, SparseCore 0:
  65.5 17.2 all-gather.11
  91.2 128.4 all-reduce.1
  295.3 60.6 reduce-scatter.1
Sparse Core Ops, SparseCore 1:
  94.0 62.4 all-gather.5
  158.8 60.7 all-gather.9
  221.9 60.8 all-gather.7
where the time goes:
time: 365 us
  waiting for transfers between devices  257 us (70%)
  local copies, waits for them, and re-layouts  37.7 us (10%)
  matrix products  28.6 us (8%)
  other arithmetic  21.5 us (6%)
  between operations  16.6 us (5%)
  blocking collectives  3.81 us (1%)
    psum x1, waiting for transfers between devices, on_device(): resid = lax.psum(contrib, ('kv', 'blk'))  127 us
    reduce_scatter x1, waiting for transfers between devices, on_device(): lax.psum_scatter(jnp.dot(hidden, down_full, preferred_element_type=jnp.fl...  60.8 us
    all_gather x1, waiting for transfers between devices, on_device(): lax.all_gather(w_up, 'req', axis=0, tiled=True)  53.8 us
    gather x1, local copies, waits for them, and re-layouts, on_device(): fresh_keys[chosen]  15 us
    gather x1, local copies, waits for them, and re-layouts, on_device(): v_new[0][chosen]  15 us
    all_gather x1, waiting for transfers between devices, combined_all(): gathered = jax.tree.map(lambda a: lax.all_gather(a, axis), part)  13.5 us
    dot_general x1, matrix products, on_device(): jnp.dot(hidden, down_full, preferred_element_type=jnp.float32)  12.4 us
  transfers between devices with their start and end apart: 6, of which 4 were waited for; matrix products, arithmetic and copies ran while one was open for 2% of the time, Pallas kernels for 0%

commit v1 on v0

--- a/solution.py
+++ b/solution.py
@@ -140,7 +140,11 @@
         preferred_element_type=jnp.float32,
     )
     up_val = jnp.dot(
-        normed, lax.all_gather(w_up, "req", axis=0, tiled=True), preferred_element_type=jnp.float32
+        normed,
+        jnp.concatenate(
+            lax.all_to_all(jnp.stack([w_up] * lax.axis_size("req")), "req", 0, 0), axis=0
+        ),
+        preferred_element_type=jnp.float32,
     )
     hidden = (jax.nn.silu(gate_val) * up_val).astype(jnp.bfloat16)
     down_full = fetch_down(w_down)

time: 365 us -> 352 us (0.964)
  waiting for transfers between devices: 257 us -> 232 us
  starting transfers between devices: 0.25 us -> 7.6 us
    all_gather x1 -> x0, waiting for transfers between devices: 53.8 us -> none  [on_device(): lax.all_gather(w_up, 'req', axis=0, tiled=True)]
    all_gather x1, waiting for transfers between devices: 0.03 us -> 38.7 us  [fetch_down(): return lax.all_gather(w_down, 'req', axis=1, tiled=True)]
    psum x1, waiting for transfers between devices: 127 us -> 118 us  [on_device(): resid = lax.psum(contrib, ('kv', 'blk'))]
    all_to_all x0 -> x1, starting transfers between devices: none -> 7.4 us  [on_device(): lax.all_to_all(jnp.stack([w_up] * lax.axis_size('req')), 'req', 0, 0)]
  transfers between devices with their start and end apart: 6 -> 6, of which waited for: 4 -> 4; matrix products, arithmetic and copies ran while one was open for 2% -> 3% of each run, Pallas kernels for 0% -> 0%
where the time goes in v1:
time: 352 us; the launch traced here: 351 us
  waiting for transfers between devices  232 us (66%)
  local copies, waits for them, and re-layouts  40.5 us (12%)
  matrix products  28.9 us (8%)
  other arithmetic  21.6 us (6%)
  between operations  16.4 us (5%)
  starting transfers between devices  7.6 us (2%)
  blocking collectives  3.81 us (1%)
    psum x1, waiting for transfers between devices, on_device(): resid = lax.psum(contrib, ('kv', 'blk'))  118 us
    reduce_scatter x1, waiting for transfers between devices, on_device(): lax.psum_scatter(jnp.dot(hidden, down_full, preferred_element_type=jnp.fl...  60.8 us
    all_gather x1, waiting for transfers between devices, fetch_down(): return lax.all_gather(w_down, 'req', axis=1, tiled=True)  38.7 us
    gather x1, local copies, waits for them, and re-layouts, on_device(): fresh_keys[chosen]  15 us
    gather x1, local copies, waits for them, and re-layouts, on_device(): v_new[0][chosen]  15 us
    all_gather x1, waiting for transfers between devices, combined_all(): gathered = jax.tree.map(lambda a: lax.all_gather(a, axis), part)  13.5 us
    dot_general x1, matrix products, on_device(): jnp.dot(hidden, down_full, preferred_element_type=jnp.float32)  12.5 us
    all_to_all x1, starting transfers between devices, on_device(): lax.all_to_all(jnp.stack([w_up] * lax.axis_size('req')), 'req', 0, 0)  7.4 us
  transfers between devices with their start and end apart: 6, of which 4 were waited for; matrix products, arithmetic and copies ran while one was open for 3% of the time, Pallas kernels for 0%

profile of v1, /device:TPU:2, one launch (start us, length us, event | category | flops | bytes accessed | tf_op | source)
XLA Modules:
  0.0 351.1 jit_solution(7333776123338255573)
XLA Ops:
  8.9 0.9 copy.31
  10.3 0.8 select_reduce_fusion
  11.4 1.9 reshape.301
  13.3 1.3 copy.30
  14.8 15.0 %gather_fusion = bf16[4096,128]{1,0:T(8,128)(2,1)} fusion(bf16[256,128]{1,0:T(8,128)(2,1)S(1)} %copy.32, s32[4096]{0:T(1024)S(1)} %broadcast_clamp_fusion), kind=kCustom, calls=%fused_computation | custom fusion | bytes 2113536 | tf_op jit(solution)/shard_map/gather | solution.py:104
  29.8 15.0 %gather_fusion.1 = bf16[4096,128]{1,0:T(8,128)(2,1)} fusion(bf16[256,128]{1,0:T(8,128)(2,1)S(1)} %bitcast.88, s32[4096]{0:T(1024)S(1)} %broadcast_clamp_fusion), kind=kCustom, calls=%fused_computation.1 | custom fusion | bytes 2113536 | tf_op jit(solution)/shard_map/gather | solution.py:107
  44.9 0.6 broadcast_compare_fusion
  45.6 3.6 %bitcast_select_fusion.2 = bf16[4096,128]{1,0:T(8,128)(2,1)S(1)} fusion(bf16[4096,128]{1,0:T(8,128)(2,1)} %gather_fusion, bf16[1,1,32,128,128]{4,3,2,1,0:T(8,128)(2,1)} %param.17, pred[4096]{0:T(1024)(128)(4,1)S(1)} %compare_and_fusion), kind=kLoop, calls=%fused_computation.13 | loop fusion | flops 524288 | bytes 3149824 | tf_op jit(solution)/shard_map/jit(_where)/select_n | solution.py:103
  49.2 3.7 %fusion.1 = (f32[1024]{0:T(1024)S(1)}, f32[1024,4096]{1,0:T(8,128)S(1)}) fusion(pred[256,4096]{1,0:T(8,128)(4,1)S(1)} %broadcast_compare_fusion, bf16[4096,128]{1,0:T(8,128)(2,1)S(1)} %bitcast_select_fusion.2, bf16[1024,64]{0,1:T(8,128)(2,1)S(1)} %bitcast.96, bf16[1024,64]{0,1:T(8,128)(2,1)S(1)} %bitcast.95), kind=kOutput, calls=%fused_computation.6 | convolution fusion | flops 1086848000 | bytes 19140608 | tf_op jit(solution)/shard_map/qd,sd->qs/dot_general | solution.py:109
  52.9 6.7 %convert_reduce_fusion = (f32[1024]{0:T(1024)S(1)}, bf16[1024,4096]{1,0:T(8,128)(2,1)S(1)}) fusion(f32[1024]{0:T(1024)S(1)} %get-tuple-element.46, f32[1024,4096]{1,0:T(8,128)S(1)} %get-tuple-element.47, pred[256,4096]{1,0:T(8,128)(4,1)S(1)} %broadcast_compare_fusion), kind=kLoop, calls=%fused_computation.5 | loop fusion | flops 29359104 | bytes 26222592 | tf_op jit(solution)/shard_map/reduce_sum | solution.py:120
  59.7 1.5 broadcast_select_fusion
  61.2 1.0 copy-done.7
  62.2 3.2 fusion.34
  65.4 1.8 all_gather.29
  67.3 2.0 all_gather.25
  69.3 13.5 %all-gather.9.cloned.1.call-done = f32[8,256,128]{2,1,0:T(8,128)} async-done(((f32[4,256,128]{2,1,0:T(8,128)}), f32[8,256,128]{2,1,0:T(8,128)}) %all-gather.9.cloned.1.call-update) | async-done | bytes 1048592 | tf_op jit(solution)/shard_map/all_gather | solution.py:9
  82.8 1.3 fusion.33
  84.1 0.8 copy.37
  85.1 1.0 divide_convert_fusion
  86.1 3.3 fusion.35
  89.4 1.8 fusion.8
  91.3 0.5 all-gather.5.cloned.1.call-update
  91.8 0.5 all-gather.7.cloned.1.call-update
  92.4 2.8 stack.2
  95.2 7.4 %all-to-all-start = ((bf16[16,320,448]{2,1,0:T(8,128)(2,1)}), bf16[16,320,448]{2,1,0:T(8,128)(2,1)}, u32[]{:S(2)}, u32[]{:S(2)}) async-start(bf16[16,320,448]{2,1,0:T(8,128)(2,1)} %stack.2), calls=%async_computation | async-start | bytes 10485760 | tf_op jit(solution)/shard_map/all_to_all | solution.py:145
  102.7 118.1 %all-reduce.2.cloned.1.call-done = f32[256,5120]{1,0:T(8,128)} async-done(((f32[256,5120]{1,0:T(8,128)}), f32[256,5120]{1,0:T(8,128)}) %all-reduce.2.cloned.1.call-update) | async-done | bytes 5242896 | tf_op jit(solution)/shard_map/psum | solution.py:134
  220.8 3.0 multiply_reduce_fusion
  223.9 6.3 %fusion.29 = f32[256,448]{0,1:T(8,128)S(1)} fusion(bf16[5120,448]{1,0:T(8,128)(2,1)} %all-gather.5.cloned.1.call-done, f32[256,5120]{1,0:T(8,128)} %all-reduce.2.cloned.1.call-done, f32[5120]{0:T(1024)S(1)} %convert_element_type.69, f32[256]{0:T(256)S(1)} %add_rsqrt_fusion), kind=kOutput, calls=%fused_computation.74 | convolution fusion | flops 1178337280 | bytes 10310656 | tf_op jit(solution)/shard_map/dot_general | solution.py:137
  230.1 38.7 %all-gather.7.cloned.1.call-done = bf16[448,5120]{0,1:T(8,128)(2,1)} async-done(((bf16[448,320]{0,1:T(8,128)(2,1)}), bf16[448,5120]{0,1:T(8,128)(2,1)}) %all-gather.7.cloned.1.call-update) | async-done | bytes 4587536 | tf_op jit(solution)/shard_map/all_gather | solution.py:51
  268.9 12.5 %convolution_convert_fusion = bf16[256,5120]{1,0:T(8,128)(2,1)} fusion(bf16[448,5120]{0,1:T(8,128)(2,1)} %all-gather.7.cloned.1.call-done, bf16[5120,448]{1,0:T(8,128)(2,1)} %bitcast.22, f32[256,448]{0,1:T(8,128)S(1)} %fusion.29, f32[256,5120]{1,0:T(8,128)} %all-reduce.2.cloned.1.call-done, f32[5120]{0:T(1024)S(1)} %convert_element_type.69, ...), kind=kOutput, calls=%fused_computation.7 | convolution fusion | flops 2354741248 | bytes 17519616 | tf_op jit(solution)/shard_map/dot_general | solution.py:152
  281.4 60.8 %reduce-scatter.2.cloned.1.call-done = bf16[16,5120]{1,0:T(8,128)(2,1)} async-done(((bf16[256,5120]{1,0:T(8,128)(2,1)}), bf16[16,5120]{1,0:T(8,128)(2,1)}) %reduce-scatter.2.cloned.1.call-update) | async-done | bytes 163856 | tf_op jit(solution)/shard_map/reduce_scatter | solution.py:151
  342.3 1.8 fusion.14
  (58 shorter events, 1.5 us)
Async XLA Ops:
  8.0 78.1 %copy-start = (bf16[256,5120]{1,0:T(8,128)(2,1)S(1)}, bf16[256,5120]{1,0:T(8,128)(2,1)}, u32[]{:S(2)}) copy-start(bf16[256,5120]{1,0:T(8,128)(2,1)} %param.21) | copy-start | bytes 7864324
  8.0 74.8 %all-gather.9.cloned.1.call-start = ((), (), s32[]{:S(2)}) async-start(), calls=%async_computation.6 | async-start | bytes 1572864 | tf_op jit(solution)/shard_map/all_gather | solution.py:9
  14.6 15.2 %copy-start.2 = (bf16[1,256,128]{2,1,0:T(8,128)(2,1)S(1)}, bf16[1,256,128]{2,1,0:T(8,128)(2,1)}, u32[]{:S(2)}) copy-start(bf16[1,256,128]{2,1,0:T(8,128)(2,1)} %param.16) | copy-start | bytes 196612
  52.9 6.8 %copy-start.3 = (bf16[4096,128]{1,0:T(8,128)(2,1)S(1)}, bf16[4096,128]{1,0:T(8,128)(2,1)}, u32[]{:S(2)}) copy-start(bf16[4096,128]{1,0:T(8,128)(2,1)} %gather_fusion) | copy-start | bytes 3145732
  52.9 6.8 %copy-start.4 = (bf16[4096,128]{1,0:T(8,128)(2,1)S(1)}, bf16[4096,128]{1,0:T(8,128)(2,1)}, u32[]{:S(2)}) copy-start(bf16[4096,128]{1,0:T(8,128)(2,1)} %gather_fusion.1) | copy-start | bytes 3145732
  52.9 6.8 %copy-start.5 = (bf16[1,1,32,128,128]{4,3,2,1,0:T(8,128)(2,1)S(1)}, bf16[1,1,32,128,128]{4,3,2,1,0:T(8,128)(2,1)}, u32[]{:S(2)}) copy-start(bf16[1,1,32,128,128]{4,3,2,1,0:T(8,128)(2,1)} %param.17) | copy-start | bytes 3145732
  52.9 6.8 %copy-start.6 = (bf16[1,1,32,128,128]{4,3,2,1,0:T(8,128)(2,1)S(1)}, bf16[1,1,32,128,128]{4,3,2,1,0:T(8,128)(2,1)}, u32[]{:S(2)}) copy-start(bf16[1,1,32,128,128]{4,3,2,1,0:T(8,128)(2,1)} %param.18) | copy-start | bytes 3145732
  61.2 1.0 copy-start.7
  65.3 155.5 %all-reduce.2.cloned.1.call-start = ((), (), s32[]{:S(2)}) async-start(), calls=%async_computation.2 | async-start | bytes 10485760 | tf_op jit(solution)/shard_map/psum | solution.py:134
  85.0 4.4 %copy-start.9 = (bf16[1,16,5120]{2,1,0:T(8,128)(2,1)S(1)}, bf16[1,16,5120]{2,1,0:T(8,128)(2,1)}, u32[]{:S(2)}) copy-start(bf16[1,16,5120]{2,1,0:T(8,128)(2,1)} %param.13) | copy-start | bytes 491524
  89.4 3.0 copy-start.8
  91.2 132.6 %all-gather.5.cloned.1.call-start = ((), (), s32[]{:S(2)}) async-start(), calls=%async_computation.3 | async-start | bytes 5570560 | tf_op jit(solution)/shard_map/all_gather | solution.py:139
  91.8 177.1 %all-gather.7.cloned.1.call-start = ((), (), s32[]{:S(2)}) async-start(), calls=%async_computation.4 | async-start | bytes 5570560 | tf_op jit(solution)/shard_map/all_gather | solution.py:51
  95.2 7.5 %copy-start.10 = (bf16[5120]{0:T(1024)(128)(2,1)S(1)}, bf16[5120]{0:T(1024)(128)(2,1)}, u32[]{:S(2)}) copy-start(bf16[5120]{0:T(1024)(128)(2,1)} %param.22) | copy-start | bytes 30724
  95.2 134.9 %all-to-all-start = ((bf16[16,320,448]{2,1,0:T(8,128)(2,1)}), bf16[16,320,448]{2,1,0:T(8,128)(2,1)}, u32[]{:S(2)}, u32[]{:S(2)}) async-start(bf16[16,320,448]{2,1,0:T(8,128)(2,1)} %stack.2), calls=%async_computation | async-start | bytes 10485760 | tf_op jit(solution)/shard_map/all_to_all | solution.py:145
  102.6 239.6 %reduce-scatter.2.cloned.1.call-start = ((), (), s32[]{:S(2)}) async-start(), calls=%async_computation.5 | async-start | bytes 2785280 | tf_op jit(solution)/shard_map/reduce_scatter | solution.py:151
  268.9 75.1 %copy-start.1 = (bf16[256,5120]{1,0:T(8,128)(2,1)S(1)}, bf16[256,5120]{1,0:T(8,128)(2,1)}, u32[]{:S(2)}) copy-start(bf16[256,5120]{1,0:T(8,128)(2,1)} %param.21) | copy-start | bytes 7864324
Sparse Core Ops, SparseCore 0:
  65.5 17.2 all-gather.8
  91.3 129.4 all-reduce.1
  281.5 60.6 reduce-scatter.1
Sparse Core Ops, SparseCore 1:
  94.1 109.6 all-gather.4
  206.0 62.8 all-gather.6
